TPU v7x, 256 devices: a whole 4x4x8 slice. The times are simulated.
256 devices in a mesh: dp: 4 (over x), expert: 32 (over z, y), tensor: 2 (over core).
Axes of the slice: x: 4, y: 4, z: 8, core: 2. Of those that a mesh axis runs over, the one named last changes fastest.
Arguments:
- queries: bfloat16 [8192, 4096], P(('dp', 'expert'), 'tensor'), may hold values from -8 to 8
- fresh_keys: bfloat16 [8192, 512], P(('dp', 'expert'), 'tensor'), may hold values from -6 to 6
- fresh_values: bfloat16 [8192, 512], P(('dp', 'expert'), 'tensor'), may hold values from -6 to 6
- resident_keys: bfloat16 [128, 2048, 512], P(('dp', 'expert'), None, 'tensor'), may hold values from -8 to 8
- resident_values: bfloat16 [128, 2048, 512], P(('dp', 'expert'), None, 'tensor'), may hold values from -6 to 6
- out_weight: bfloat16 [4096, 2048], P('tensor', 'dp'), may hold values from -0.5 to 0.5
- residual: bfloat16 [8192, 2048], P(('dp', 'expert')), may hold values from -23 to 23
- norm_gain: float32 [2048], replicated, may hold values from 0.1 to 1.9
- expert_ids: int32 [8192, 8], P(('dp', 'expert')), may hold values from 0 to 127, all different within a row; in each aligned block of 64 rows (0 to 63, 64 to 127, ...) at most 6 rows name the same one
- gates: float32 [8192, 8], P(('dp', 'expert')), may hold values from 0.05 to 0.5
- w_gate: bfloat16 [128, 2048, 768], P(('dp', 'expert'), None, 'tensor'), may hold values from -0.125 to 0.125
- w_up: bfloat16 [128, 2048, 768], P(('dp', 'expert'), None, 'tensor'), may hold values from -0.125 to 0.125
- w_down: bfloat16 [128, 768, 2048], P(('dp', 'expert'), 'tensor'), may hold values from -0.21875 to 0.21875
Outputs:
- mixed: bfloat16 [8192, 2048], P(('dp', 'expert'), 'tensor')
Inputs may be any that keep to these rules, and one draw needn't show every extreme that they name: `expert_ids`: within the 64 tokens of one sequence no expert is named by more than 6 tokens, a bound that some block reaches; a token names 8 different experts.
All inputs are finite; a program needn't handle non-finite values.
Results may differ from a plain program's by a relative error of at most 0.0085.
Values may be sent and summed in bfloat16 or wider, within the bound.
No kernel may reach another device: no remote copies, remote signals or barrier semaphores. Data moves between devices by JAX's collectives and lax.ppermute only.
A program may use at most 64 MiB of HBM per device.

v0:
```python
import jax
import jax.numpy as jnp
from jax import lax
from jax.sharding import PartitionSpec as P

D = 2048
HEAD_WIDTH = 128
CAP = 6


def attend_local(queries, fresh_keys, fresh_values, resident_keys, resident_values):
    tokens_here = queries.shape[0]
    kv_here = fresh_keys.shape[1] // HEAD_WIDTH
    query_group = queries.shape[1] // HEAD_WIDTH // kv_here
    context = resident_keys.shape[1]
    query_rows = queries.reshape(tokens_here, kv_here, query_group, HEAD_WIDTH)
    joined_keys = jnp.concatenate([resident_keys[0], fresh_keys], 0).reshape(
        context + tokens_here, kv_here, HEAD_WIDTH
    )
    joined_values = jnp.concatenate([resident_values[0], fresh_values], 0).reshape(
        context + tokens_here, kv_here, HEAD_WIDTH
    )
    score = jnp.einsum(
        "tjgd,sjd->jgts", query_rows, joined_keys, preferred_element_type=jnp.float32
    ) * HEAD_WIDTH ** (-0.5)
    places = jnp.arange(context + tokens_here)
    rows = jnp.arange(tokens_here)
    allowed = (places[None, :] < context) | (places[None, :] - context <= rows[:, None])
    score = jnp.where(allowed, score, jnp.float32(-1e30))
    top_score = jnp.max(score, axis=-1, keepdims=True)
    weight = jnp.exp(score - top_score)
    probs = (weight / jnp.sum(weight, axis=-1, keepdims=True)).astype(jnp.bfloat16)
    attended = jnp.einsum(
        "jgts,sjd->tjgd", probs, joined_values, preferred_element_type=jnp.float32
    )
    return attended.reshape(tokens_here, -1).astype(jnp.bfloat16)


def swap_pair(x):
    return lax.ppermute(x, "tensor", [(0, 1), (1, 0)])


def per_device(
    queries,
    fresh_keys,
    fresh_values,
    resident_keys,
    resident_values,
    out_weight,
    residual,
    norm_gain,
    expert_ids,
    gates,
    w_gate,
    w_up,
    w_down,
):
    tokens_here = residual.shape[0]
    lane = lax.axis_index("tensor")
    half = D // lax.axis_size("tensor")
    groups = lax.axis_size("dp")
    attended = attend_local(queries, fresh_keys, fresh_values, resident_keys, resident_values)
    gathered = lax.all_gather(attended, "dp", axis=0, tiled=True)
    part = jnp.dot(gathered, out_weight, preferred_element_type=jnp.float32)
    part = part.reshape(groups, tokens_here, -1)
    mine = lax.all_to_all(part, "dp", split_axis=0, concat_axis=0, tiled=True)
    mine = mine.transpose(1, 0, 2).reshape(tokens_here, D)
    summed = mine + swap_pair(mine)
    hidden = residual.astype(jnp.float32) + summed
    mean_square = jnp.mean(hidden * hidden, axis=-1, keepdims=True)
    normed = (hidden * lax.rsqrt(mean_square + 1e-06) * norm_gain).astype(jnp.bfloat16)
    hidden_half = lax.dynamic_slice_in_dim(hidden, lane * half, half, 1)
    normed_half = lax.dynamic_slice_in_dim(normed, lane * half, half, 1)
    owners = lax.axis_size("dp") * lax.axis_size("expert")
    onehot = (expert_ids[:, :, None] == jnp.arange(owners)[None, None, :]).astype(jnp.int32)
    per_token = jnp.sum(onehot, axis=1)
    before = jnp.cumsum(per_token, axis=0) - per_token
    slot = jnp.sum(onehot * before[:, None, :], axis=-1)
    code = expert_ids * CAP + slot
    pick = (code[:, :, None] == jnp.arange(owners * CAP)[None, None, :]).astype(jnp.bfloat16)
    spread = jnp.sum(pick, axis=1)
    outgoing = jnp.einsum(
        "tr,tf->rf", spread, normed_half, preferred_element_type=jnp.float32
    ).astype(jnp.bfloat16)
    received = lax.all_to_all(
        outgoing.reshape(owners, CAP, half),
        ("dp", "expert"),
        split_axis=0,
        concat_axis=0,
        tiled=True,
    ).reshape(owners * CAP, half)
    other = swap_pair(received)
    first = jnp.where(lane == 0, received, other)
    second = jnp.where(lane == 0, other, received)
    flat = jnp.concatenate([first, second], axis=1)
    gate_part = jnp.dot(flat, w_gate[0], preferred_element_type=jnp.float32)
    up_part = jnp.dot(flat, w_up[0], preferred_element_type=jnp.float32)
    act = (jax.nn.silu(gate_part) * up_part).astype(jnp.bfloat16)
    result = jnp.dot(act, w_down[0], preferred_element_type=jnp.float32)
    own = lax.dynamic_slice_in_dim(result, lane * half, half, 1)
    theirs = lax.dynamic_slice_in_dim(result, (1 - lane) * half, half, 1)
    expert_out = (own + swap_pair(theirs)).astype(jnp.bfloat16)
    returned = lax.all_to_all(
        expert_out.reshape(owners, CAP, half),
        ("dp", "expert"),
        split_axis=0,
        concat_axis=0,
        tiled=True,
    ).reshape(owners * CAP, half)
    picked = jnp.einsum("tkr,rf->tkf", pick, returned, preferred_element_type=jnp.float32)
    moe = jnp.sum(gates[:, :, None] * picked, axis=1)
    return (hidden_half + moe).astype(jnp.bfloat16)


def solution(mesh):
    return jax.shard_map(
        per_device,
        mesh=mesh,
        in_specs=(
            P(("dp", "expert"), "tensor"),
            P(("dp", "expert"), "tensor"),
            P(("dp", "expert"), "tensor"),
            P(("dp", "expert"), None, "tensor"),
            P(("dp", "expert"), None, "tensor"),
            P("tensor", "dp"),
            P(("dp", "expert"), None),
            P(),
            P(("dp", "expert"), None),
            P(("dp", "expert"), None),
            P(("dp", "expert"), None, "tensor"),
            P(("dp", "expert"), None, "tensor"),
            P(("dp", "expert"), "tensor", None),
        ),
        out_specs=P(("dp", "expert"), "tensor"),
        check_vma=False,
    )
```

profile of v0, /device:TPU:2, one launch (start us, length us, event | category | flops | bytes accessed | tf_op | source)
XLA Modules:
  0.0 256.4 jit_solution(13007185668899665555)
XLA Ops:
  6.5 0.0 copy-start
  6.5 0.0 all-gather.2.cloned.1.call-start
  6.5 0.6 iota_add_fusion
  7.1 1.5 copy.47
  8.7 1.3 copy.48
  10.0 0.0 copy-done.5
  10.0 0.8 copy.62
  10.8 1.5 copy.44
  12.3 1.3 copy.45
  13.7 0.0 copy-done.8
  13.7 0.0 copy-done.9
  13.7 0.6 copy_bitcast_fusion.1
  14.3 0.8 fusion.27
  15.1 0.0 copy-done.6
  15.1 0.0 copy-start.4
  15.1 4.7 %fusion.48 = f32[2,8,64]{2,1,0:T(8,128)S(1)} fusion(pred[64,2112]{1,0:T(8,128)(4,1)S(1)} %fusion.27, bf16[64,2,128]{2,0,1:T(8,128)(2,1)} %get-tuple-element.9, bf16[2048,2,128]{2,0,1:T(8,128)(2,1)} %copy.48, bf16[64,2,8,128]{3,2,1,0:T(8,128)(2,1)S(1)} %bitcast.82), kind=kOutput, calls=%fused_computation.65 | convolution fusion | flops 564463680 | bytes 1482752 | tf_op jit(solution)/shard_map/sub | solution.py:31
  19.8 0.0 copy-done.4
  19.8 5.6 %fusion.14 = bf16[64,2,8,128]{3,0,2,1:T(8,128)(2,1)} fusion(f32[2,8,64]{2,1,0:T(8,128)S(1)} %fusion.48, bf16[64,2,128]{2,0,1:T(8,128)(2,1)} %get-tuple-element.10, bf16[2048,2,128]{2,0,1:T(8,128)(2,1)} %copy.45, pred[64,2112]{1,0:T(8,128)(4,1)S(1)} %fusion.27, bf16[64,2,128]{2,0,1:T(8,128)(2,1)} %get-tuple-element.9, ...), kind=kOutput, calls=%fused_computation.25 | convolution fusion | flops 1122569216 | bytes 2826240 | tf_op jit(solution)/shard_map/jgts,sjd->tjgd/dot_general | solution.py:33
  25.4 1.1 copy.51
  26.5 0.8 copy.78
  27.3 0.0 all-gather.2.cloned.1.call-update
  27.3 0.0 copy-start.10
  27.4 28.6 %all-gather.2.cloned.1.call-done = bf16[256,2048]{1,0:T(8,128)(2,1)} async-done(((bf16[64,2048]{1,0:T(8,128)(2,1)}), bf16[256,2048]{1,0:T(8,128)(2,1)}) %all-gather.2.cloned.1.call-update) | async-done | bytes 1048592 | tf_op jit(solution)/shard_map/all_gather | solution.py:63
  55.9 0.0 copy-done
  55.9 2.7 %fusion.51 = f32[256,512]{1,0:T(8,128)} fusion(bf16[256,2048]{1,0:T(8,128)(2,1)} %all-gather.2.cloned.1.call-done, bf16[2048,512]{1,0:T(8,128)(2,1)S(1)} %copy-done), kind=kOutput, calls=%fused_computation.66 | convolution fusion | flops 536870912 | bytes 3670016 | tf_op jit(solution)/shard_map/dot_general | solution.py:64
  58.7 5.3 %all-to-all-start = ((f32[4,64,512]{2,1,0:T(8,128)}), f32[4,64,512]{2,1,0:T(8,128)S(1)}, u32[]{:S(2)}, u32[]{:S(2)}) async-start(f32[4,64,512]{2,1,0:T(8,128)} %bitcast.8), calls=%async_computation | async-start | bytes 1048576 | tf_op jit(solution)/shard_map/all_to_all | solution.py:66
  63.9 0.0 copy-done.10
  64.0 0.1 copy.54
  64.0 6.5 %all-to-all-done = f32[4,64,512]{2,1,0:T(8,128)S(1)} async-done(((f32[4,64,512]{2,1,0:T(8,128)}), f32[4,64,512]{2,1,0:T(8,128)S(1)}, u32[]{:S(2)}, u32[]{:S(2)}) %all-to-all-start) | async-done | bytes 524320 | tf_op jit(solution)/shard_map/all_to_all | solution.py:66
  70.6 0.3 collective-permute-start
  70.9 0.1 convert_reduce_fusion
  71.1 0.1 reduce_window_sum.11
  71.2 1.2 select_reduce_fusion
  72.4 0.1 copy.55
  72.5 0.1 copy.56
  72.6 0.0 copy-done.12
  72.6 0.5 fusion.19
  73.1 0.0 collective-permute-done
  73.1 0.0 copy-done.7
  73.2 1.2 multiply_reduce_fusion.1
  74.4 1.8 convolution_convert_fusion
  76.2 3.7 %reshape.67 = bf16[128,6,1024]{2,1,0:T(8,128)(2,1)} reshape(bf16[768,1024]{1,0:T(8,128)(2,1)} %convolution_convert_fusion) | data formatting | bytes 3145728 | tf_op jit(solution)/shard_map/reshape | solution.py:86
  79.9 64.9 %all_to_all.15 = bf16[128,6,1024]{2,1,0:T(8,128)(2,1)} all-to-all(bf16[128,6,1024]{2,1,0:T(8,128)(2,1)} %reshape.67), channel_id=1, replica_groups=mesh['dp'=4,'expert'=32,'tensor'=2] {'dp','expert'}, dimensions={0} | all-to-all | bytes 3145728 | tf_op jit(solution)/shard_map/all_to_all | solution.py:85
  144.8 3.7 %reshape.68 = bf16[768,1024]{1,0:T(8,128)(2,1)} reshape(bf16[128,6,1024]{2,1,0:T(8,128)(2,1)} %all_to_all.15) | data formatting | bytes 3145728 | tf_op jit(solution)/shard_map/reshape | solution.py:91
  148.5 0.0 collective-permute-start.1
  148.5 3.7 %collective-permute-done.1 = bf16[768,1024]{1,0:T(8,128)(2,1)} collective-permute-done((bf16[768,1024]{1,0:T(8,128)(2,1)}, bf16[768,1024]{1,0:T(8,128)(2,1)}, u32[]{:S(2)}, u32[]{:S(2)}) %collective-permute-start.1) | collective-permute-done | bytes 1572896 | tf_op jit(solution)/shard_map/ppermute | solution.py:40
  152.3 2.1 broadcast_select_fusion.1
  154.4 1.2 copy-done.2
  155.6 0.4 copy-done.3
  156.0 2.8 %fusion.6 = f32[768,384]{1,0:T(8,128)} fusion(bf16[768,1024]{1,0:T(8,128)(2,1)S(1)} %get-tuple-element.8, bf16[768,1024]{1,0:T(8,128)(2,1)S(1)} %get-tuple-element.7, bf16[1,2048,384]{2,1,0:T(8,128)(2,1)S(1)} %copy-done.13), kind=kOutput, calls=%fused_computation.12 | convolution fusion | flops 1214251008 | bytes 5898240 | tf_op jit(solution)/shard_map/dot_general | solution.py:97
  158.8 9.3 %fusion.8 = f32[768,2048]{1,0:T(8,128)} fusion(bf16[1,384,2048]{2,1,0:T(8,128)(2,1)} %param.25, f32[768,384]{1,0:T(8,128)} %fusion.6, bf16[768,1024]{1,0:T(8,128)(2,1)} %copy-done.3, bf16[768,1024]{1,0:T(8,128)(2,1)} %copy-done.2, bf16[1,2048,384]{2,1,0:T(8,128)(2,1)} %param.23), kind=kOutput, calls=%fused_computation.15 | convolution fusion | flops 2423980032 | bytes 13762560 | tf_op jit(solution)/shard_map/dot_general | solution.py:99
  168.0 2.3 constant_dynamic-slice_fusion
  170.3 0.2 collective-permute-start.2
  170.5 5.5 %collective-permute-done.2 = f32[768,1024]{1,0:T(8,128)S(1)} collective-permute-done((f32[768,1024]{1,0:T(8,128)S(1)}, f32[768,1024]{1,0:T(8,128)S(1)}, u32[]{:S(2)}, u32[]{:S(2)}) %collective-permute-start.2) | collective-permute-done | bytes 3145760 | tf_op jit(solution)/shard_map/ppermute | solution.py:40
  176.1 0.0 copy-done.1
  176.1 1.7 add_convert_fusion
  177.7 3.7 %reshape.69 = bf16[128,6,1024]{2,1,0:T(8,128)(2,1)} reshape(bf16[768,1024]{1,0:T(8,128)(2,1)} %add_convert_fusion) | data formatting | bytes 3145728 | tf_op jit(solution)/shard_map/reshape | solution.py:104
  181.4 9.0 %all-to-all-start.2 = ((bf16[128,6,1024]{2,1,0:T(8,128)(2,1)}), bf16[128,6,1024]{2,1,0:T(8,128)(2,1)}, u32[]{:S(2)}, u32[]{:S(2)}) async-start(bf16[128,6,1024]{2,1,0:T(8,128)(2,1)} %reshape.69), calls=%async_computation.2 | async-start | bytes 4194304 | tf_op jit(solution)/shard_map/all_to_all | solution.py:103
  190.5 0.0 copy-done.11
  190.5 0.1 copy.53
  190.6 51.7 %all-to-all-done.2 = bf16[128,6,1024]{2,1,0:T(8,128)(2,1)} async-done(((bf16[128,6,1024]{2,1,0:T(8,128)(2,1)}), bf16[128,6,1024]{2,1,0:T(8,128)(2,1)}, u32[]{:S(2)}, u32[]{:S(2)}) %all-to-all-start.2) | async-done | bytes 1572896 | tf_op jit(solution)/shard_map/all_to_all | solution.py:103
  242.3 3.7 %reshape.73 = bf16[768,1024,1]{1,0,2:T(8,128)(2,1)} reshape(bf16[128,6,1024]{2,1,0:T(8,128)(2,1)} %all-to-all-done.2) | data formatting | bytes 3145728 | tf_op jit(solution)/shard_map/reshape | solution.py:109
  246.0 2.8 %multiply_reduce_fusion = f32[64,1024]{1,0:T(8,128)S(1)} fusion(bf16[768,1024,1]{1,0,2:T(8,128)(2,1)} %reshape.73, f32[64,8]{1,0:T(8,128)S(1)} %copy.53, s32[64,8]{1,0:T(8,128)S(1)} %copy.56), kind=kOutput, calls=%fused_computation.11 | convolution fusion | flops 806682624 | bytes 1839104 | tf_op jit(solution)/shard_map/tkr,rf->tkf/dot_general | solution.py:110
  248.8 0.7 add_convert_fusion.1
  (18 shorter events, 0.1 us)
Async XLA Ops:
  6.5 49.4 %copy-start = (bf16[2048,512]{1,0:T(8,128)(2,1)S(1)}, bf16[2048,512]{1,0:T(8,128)(2,1)}, u32[]{:S(2)}) copy-start(bf16[2048,512]{1,0:T(8,128)(2,1)} %param.18) | copy-start | bytes 6291460
  6.5 49.4 %all-gather.2.cloned.1.call-start = ((), (), s32[]{:S(2)}) async-start(), calls=%async_computation.3 | async-start | bytes 1310720 | tf_op jit(solution)/shard_map/all_gather | solution.py:63
  7.1 2.9 %copy-start.5 = (bf16[64,2048]{1,0:T(8,128)(2,1)S(1)}, bf16[64,2048]{1,0:T(8,128)(2,1)}, u32[]{:S(2)}) copy-start(bf16[64,2048]{1,0:T(8,128)(2,1)} %param.13) | copy-start | bytes 786436
  10.8 2.9 %copy-start.8 = (bf16[64,256]{1,0:T(8,128)(2,1)S(1)}, bf16[64,256]{1,0:T(8,128)(2,1)}, u32[]{:S(2)}) copy-start(bf16[64,256]{1,0:T(8,128)(2,1)} %param.15) | copy-start | bytes 98308
  10.8 2.9 %copy-start.9 = (bf16[64,256]{1,0:T(8,128)(2,1)S(1)}, bf16[64,256]{1,0:T(8,128)(2,1)}, u32[]{:S(2)}) copy-start(bf16[64,256]{1,0:T(8,128)(2,1)} %param.14) | copy-start | bytes 98308
  10.8 4.3 %copy-start.6 = (bf16[8,8,16,128]{3,2,1,0:T(8,128)(2,1)S(1)}, bf16[8,8,16,128]{3,2,1,0:T(8,128)(2,1)}, u32[]{:S(2)}) copy-start(bf16[8,8,16,128]{3,2,1,0:T(8,128)(2,1)} %copy.62) | copy-start | bytes 786436
  15.1 4.7 %copy-start.4 = (bf16[2048,2,128]{2,0,1:T(8,128)(2,1)S(1)}, bf16[2048,2,128]{2,0,1:T(8,128)(2,1)}, u32[]{:S(2)}) copy-start(bf16[2048,2,128]{2,0,1:T(8,128)(2,1)} %copy.48) | copy-start | bytes 3145732
  27.3 36.6 %copy-start.10 = (s32[64,8]{0,1:T(8,128)S(1)}, s32[64,8]{0,1:T(8,128)}, u32[]{:S(2)}) copy-start(s32[64,8]{0,1:T(8,128)} %param.21) | copy-start | bytes 6148
  58.7 13.9 %copy-start.12 = (f32[2048]{0:T(1024)S(1)}, f32[2048]{0:T(1024)}, u32[]{:S(2)}) copy-start(f32[2048]{0:T(1024)} %param.20) | copy-start | bytes 24580
  58.7 14.5 %copy-start.7 = (bf16[64,2048]{1,0:T(8,128)(2,1)S(1)}, bf16[64,2048]{1,0:T(8,128)(2,1)}, u32[]{:S(2)}) copy-start(bf16[64,2048]{1,0:T(8,128)(2,1)} %param.19) | copy-start | bytes 786436
  58.7 11.9 %all-to-all-start = ((f32[4,64,512]{2,1,0:T(8,128)}), f32[4,64,512]{2,1,0:T(8,128)S(1)}, u32[]{:S(2)}, u32[]{:S(2)}) async-start(f32[4,64,512]{2,1,0:T(8,128)} %bitcast.8), calls=%async_computation | async-start | bytes 1048576 | tf_op jit(solution)/shard_map/all_to_all | solution.py:66
  70.6 2.5 collective-permute-start
  148.5 3.8 %collective-permute-start.1 = (bf16[768,1024]{1,0:T(8,128)(2,1)}, bf16[768,1024]{1,0:T(8,128)(2,1)}, u32[]{:S(2)}, u32[]{:S(2)}) collective-permute-start(bf16[768,1024]{1,0:T(8,128)(2,1)} %reshape.68), channel_id=1, source_target_pairs={{0,1},{1,0},{2,3},{3,2},{4,5},{5,4},{6,7},{7,6},{8,9},{9,8},{10,11... | collective-permute-start | bytes 4718600 | tf_op jit(solution)/shard_map/ppermute | solution.py:40
  148.5 7.5 %copy-start.13 = (bf16[1,2048,384]{2,1,0:T(8,128)(2,1)S(1)}, bf16[1,2048,384]{2,1,0:T(8,128)(2,1)}, u32[]{:S(2)}) copy-start(bf16[1,2048,384]{2,1,0:T(8,128)(2,1)} %param.24) | copy-start | bytes 4718596
  154.3 1.2 copy-start.2
  154.4 1.6 copy-start.3
  168.0 8.0 %copy-start.1 = (f32[768,2048]{1,0:T(8,128)S(1)}, f32[768,2048]{1,0:T(8,128)}, u32[]{:S(2)}) copy-start(f32[768,2048]{1,0:T(8,128)} %fusion.8) | copy-start | bytes 18874372
  170.3 5.7 %collective-permute-start.2 = (f32[768,1024]{1,0:T(8,128)S(1)}, f32[768,1024]{1,0:T(8,128)S(1)}, u32[]{:S(2)}, u32[]{:S(2)}) collective-permute-start(f32[768,1024]{1,0:T(8,128)S(1)} %constant_dynamic-slice_fusion), channel_id=1, source_target_pairs={{0,1},{1,0},{2,3},{3,2},{4,5},{5,4},{6,7},{7,6},{8,9},{9,8},{10,11... | collective-permute-start | bytes 9437192 | tf_op jit(solution)/shard_map/ppermute | solution.py:40
  181.4 9.0 %copy-start.11 = (f32[64,8]{0,1:T(8,128)S(1)}, f32[64,8]{0,1:T(8,128)}, u32[]{:S(2)}) copy-start(f32[64,8]{0,1:T(8,128)} %param.22) | copy-start | bytes 6148
  181.4 60.9 %all-to-all-start.2 = ((bf16[128,6,1024]{2,1,0:T(8,128)(2,1)}), bf16[128,6,1024]{2,1,0:T(8,128)(2,1)}, u32[]{:S(2)}, u32[]{:S(2)}) async-start(bf16[128,6,1024]{2,1,0:T(8,128)(2,1)} %reshape.69), calls=%async_computation.2 | async-start | bytes 4194304 | tf_op jit(solution)/shard_map/all_to_all | solution.py:103
Sparse Core Ops, SparseCore 0:
  27.5 28.4 all-gather.1
where the time goes:
time: 257 us; the launch traced here: 256 us
  waiting for transfers between devices  96.2 us (37%)
  blocking collectives  64.9 us (25%)
  matrix products  29.7 us (12%)
  local copies, waits for them, and re-layouts  28.1 us (11%)
  starting transfers between devices  14.8 us (6%)
  between operations  13.6 us (5%)
  other arithmetic  9.14 us (4%)
    all_to_all x1, blocking collectives, per_device(): lax.all_to_all(outgoing.reshape(owners, CAP, half), ('dp', 'expert'), spl...  64.9 us
    all_to_all x1, waiting for transfers between devices, per_device(): lax.all_to_all(expert_out.reshape(owners, CAP, half), ('dp', 'expert'), s...  51.7 us
    all_gather x1, waiting for transfers between devices, per_device(): gathered = lax.all_gather(attended, 'dp', axis=0, tiled=True)  28.6 us
    dot_general x1, matrix products, per_device(): result = jnp.dot(act, w_down[0], preferred_element_type=jnp.float32)  9.28 us
    ppermute x3, waiting for transfers between devices, swap_pair(): return lax.ppermute(x, 'tensor', [(0, 1), (1, 0)])  9.27 us
    all_to_all x1, starting transfers between devices, per_device(): lax.all_to_all(expert_out.reshape(owners, CAP, half), ('dp', 'expert'), s...  9.03 us
    all_to_all x1, waiting for transfers between devices, per_device(): mine = lax.all_to_all(part, 'dp', split_axis=0, concat_axis=0, tiled=True)  6.54 us
    unnamed x34, local copies, waits for them, and re-layouts  6.45 us
  transfers between devices with their start and end apart: 6, of which 5 were waited for; matrix products, arithmetic and copies ran while one was open for 1% of the time, Pallas kernels for 0%

commit v1 on v0

--- a/solution.py
+++ b/solution.py
@@ -60,7 +60,22 @@
     half = D // lax.axis_size("tensor")
     groups = lax.axis_size("dp")
     attended = attend_local(queries, fresh_keys, fresh_values, resident_keys, resident_values)
-    gathered = lax.all_gather(attended, "dp", axis=0, tiled=True)
+    ways, here, step = (lax.axis_size("dp"), lax.axis_index("dp"), attended.shape[0])
+    shape = [n * ways if d == 0 else n for d, n in enumerate(attended.shape)]
+    gathered = lax.dynamic_update_slice_in_dim(
+        jnp.zeros(shape, attended.dtype), attended, here * step, axis=0
+    )
+    going_up = going_down = attended
+    for far in range(1, ways // 2 + 1):
+        going_up = lax.ppermute(going_up, "dp", [(d, (d + 1) % ways) for d in range(ways)])
+        gathered = lax.dynamic_update_slice_in_dim(
+            gathered, going_up, (here - far) % ways * step, axis=0
+        )
+        if 2 * far < ways:
+            going_down = lax.ppermute(going_down, "dp", [(d, (d - 1) % ways) for d in range(ways)])
+            gathered = lax.dynamic_update_slice_in_dim(
+                gathered, going_down, (here + far) % ways * step, axis=0
+            )
     part = jnp.dot(gathered, out_weight, preferred_element_type=jnp.float32)
     part = part.reshape(groups, tokens_here, -1)
     mine = lax.all_to_all(part, "dp", split_axis=0, concat_axis=0, tiled=True)

time: 257 us -> 233 us (0.907)
  waiting for transfers between devices: 96.2 us -> 77.1 us
  between operations: 13.6 us -> 0.3 us
  starting transfers between devices: 14.8 us -> 19.2 us
    all_gather x1 -> x0, waiting for transfers between devices: 28.6 us -> none  [per_device(): gathered = lax.all_gather(attended, 'dp', axis=0, tiled=True)]
    ppermute x0 -> x3, waiting for transfers between devices: none -> 9.57 us  [the longest x2 9.56 us: per_device(): lax.ppermute(going_up, 'dp', [(d, (d + 1) % ways) for d in range(ways)])]
    ppermute x0 -> x3, starting transfers between devices: none -> 3.74 us  [the longest x2 2.99 us: per_device(): lax.ppermute(going_up, 'dp', [(d, (d + 1) % ways) for d in range(ways)])]
  transfers between devices with their start and end apart: 6 -> 8, of which waited for: 5 -> 6; matrix products, arithmetic and copies ran while one was open for 1% -> 2% of each run, Pallas kernels for 0% -> 0%
where the time goes in v1:
time: 233 us; the launch traced here: 232 us
  waiting for transfers between devices  77.1 us (33%)
  blocking collectives  67.3 us (29%)
  local copies, waits for them, and re-layouts  30.3 us (13%)
  matrix products  28.4 us (12%)
  starting transfers between devices  19.2 us (8%)
  other arithmetic  9.14 us (4%)
    all_to_all x1, blocking collectives, per_device(): lax.all_to_all(outgoing.reshape(owners, CAP, half), ('dp', 'expert'), spl...  67.3 us
    all_to_all x1, waiting for transfers between devices, per_device(): lax.all_to_all(expert_out.reshape(owners, CAP, half), ('dp', 'expert'), s...  51.7 us
    ppermute x2, waiting for transfers between devices, per_device(): lax.ppermute(going_up, 'dp', [(d, (d + 1) % ways) for d in range(ways)])  9.56 us
    dot_general x1, matrix products, per_device(): result = jnp.dot(act, w_down[0], preferred_element_type=jnp.float32)  9.28 us
    ppermute x3, waiting for transfers between devices, swap_pair(): return lax.ppermute(x, 'tensor', [(0, 1), (1, 0)])  9.27 us
    all_to_all x1, starting transfers between devices, per_device(): lax.all_to_all(expert_out.reshape(owners, CAP, half), ('dp', 'expert'), s...  9.03 us
    all_to_all x1, waiting for transfers between devices, per_device(): mine = lax.all_to_all(part, 'dp', split_axis=0, concat_axis=0, tiled=True)  6.54 us
    unnamed x34, local copies, waits for them, and re-layouts  6.44 us
  transfers between devices with their start and end apart: 8, of which 6 were waited for; matrix products, arithmetic and copies ran while one was open for 2% of the time, Pallas kernels for 0%

profile of v1, /device:TPU:2, one launch (start us, length us, event | category | flops | bytes accessed | tf_op | source)
XLA Modules:
  0.0 231.8 jit_solution(8581107260822255794)
XLA Ops:
  0.0 0.0 copy-start
  0.0 0.6 iota_add_fusion
  0.6 1.5 copy.47
  2.1 1.3 copy.48
  3.5 0.0 copy-done.5
  3.5 0.8 copy.62
  4.3 1.5 copy.44
  5.8 1.3 copy.45
  7.1 0.0 copy-done.8
  7.1 0.0 copy-done.9
  7.1 0.6 copy_bitcast_fusion.1
  7.8 0.8 fusion.27
  8.6 4.7 %fusion.48 = f32[2,8,64]{2,1,0:T(8,128)S(1)} fusion(pred[64,2112]{1,0:T(8,128)(4,1)S(1)} %fusion.27, bf16[64,2,128]{2,0,1:T(8,128)(2,1)} %get-tuple-element.9, bf16[2048,2,128]{2,0,1:T(8,128)(2,1)} %copy.48, bf16[64,2,8,128]{3,2,1,0:T(8,128)(2,1)S(1)} %bitcast.85), kind=kOutput, calls=%fused_computation.69 | convolution fusion | flops 564463680 | bytes 1482752 | tf_op jit(solution)/shard_map/sub | solution.py:31
  13.2 5.6 %fusion.14 = bf16[64,2,8,128]{3,0,2,1:T(8,128)(2,1)} fusion(f32[2,8,64]{2,1,0:T(8,128)S(1)} %fusion.48, bf16[64,2,128]{2,0,1:T(8,128)(2,1)} %get-tuple-element.10, bf16[2048,2,128]{2,0,1:T(8,128)(2,1)} %copy.45, pred[64,2112]{1,0:T(8,128)(4,1)S(1)} %fusion.27, bf16[64,2,128]{2,0,1:T(8,128)(2,1)} %get-tuple-element.9, ...), kind=kOutput, calls=%fused_computation.25 | convolution fusion | flops 1122569216 | bytes 2826240 | tf_op jit(solution)/shard_map/jgts,sjd->tjgd/dot_general | solution.py:33
  18.9 1.1 copy.51
  20.0 0.8 copy.80
  20.8 1.5 collective-permute-start
  22.3 0.8 collective-permute-start.1
  23.0 0.1 broadcast_in_dim.10
  23.1 0.1 constant_dynamic-update-slice_fusion.3
  23.2 5.9 %collective-permute-done = bf16[64,2048]{1,0:T(8,128)(2,1)} collective-permute-done((bf16[64,2048]{1,0:T(8,128)(2,1)}, bf16[64,2048]{1,0:T(8,128)(2,1)}, u32[]{:S(2)}, u32[]{:S(2)}) %collective-permute-start) | collective-permute-done | bytes 262176 | tf_op jit(solution)/shard_map/ppermute | solution.py:70
  29.1 1.5 collective-permute-start.2
  30.6 1.0 constant_dynamic-update-slice_fusion.2
  31.6 0.0 collective-permute-done.1
  31.6 1.0 constant_dynamic-update-slice_fusion.1
  32.6 3.7 %collective-permute-done.2 = bf16[64,2048]{1,0:T(8,128)(2,1)S(1)} collective-permute-done((bf16[64,2048]{1,0:T(8,128)(2,1)}, bf16[64,2048]{1,0:T(8,128)(2,1)S(1)}, u32[]{:S(2)}, u32[]{:S(2)}) %collective-permute-start.2) | collective-permute-done | bytes 262176 | tf_op jit(solution)/shard_map/ppermute | solution.py:70
  36.3 0.0 copy-start.10
  36.4 1.5 fusion.51
  37.8 6.0 %all-to-all-start = ((f32[4,64,512]{2,1,0:T(8,128)}), f32[4,64,512]{2,1,0:T(8,128)S(1)}, u32[]{:S(2)}, u32[]{:S(2)}) async-start(f32[4,64,512]{2,1,0:T(8,128)} %bitcast.83), calls=%async_computation | async-start | bytes 1048576 | tf_op jit(solution)/shard_map/all_to_all | solution.py:81
  43.8 0.1 copy.54
  43.9 6.5 %all-to-all-done = f32[4,64,512]{2,1,0:T(8,128)S(1)} async-done(((f32[4,64,512]{2,1,0:T(8,128)}), f32[4,64,512]{2,1,0:T(8,128)S(1)}, u32[]{:S(2)}, u32[]{:S(2)}) %all-to-all-start) | async-done | bytes 524320 | tf_op jit(solution)/shard_map/all_to_all | solution.py:81
  50.5 0.3 collective-permute-start.3
  50.8 0.1 convert_reduce_fusion
  50.9 0.1 reduce_window_sum.11
  51.0 1.2 select_reduce_fusion
  52.3 0.1 copy.55
  52.3 0.1 copy.56
  52.4 0.0 copy-done.12
  52.5 0.5 fusion.19
  53.0 0.0 collective-permute-done.3
  53.0 1.2 multiply_reduce_fusion.1
  54.3 1.8 convolution_convert_fusion
  56.0 3.7 %reshape.67 = bf16[128,6,1024]{2,1,0:T(8,128)(2,1)} reshape(bf16[768,1024]{1,0:T(8,128)(2,1)} %convolution_convert_fusion) | data formatting | bytes 3145728 | tf_op jit(solution)/shard_map/reshape | solution.py:101
  59.8 67.3 %all_to_all.15 = bf16[128,6,1024]{2,1,0:T(8,128)(2,1)} all-to-all(bf16[128,6,1024]{2,1,0:T(8,128)(2,1)} %reshape.67), channel_id=1, replica_groups=mesh['dp'=4,'expert'=32,'tensor'=2] {'dp','expert'}, dimensions={0} | all-to-all | bytes 3145728 | tf_op jit(solution)/shard_map/all_to_all | solution.py:100
  127.1 3.7 %reshape.68 = bf16[768,1024]{1,0:T(8,128)(2,1)} reshape(bf16[128,6,1024]{2,1,0:T(8,128)(2,1)} %all_to_all.15) | data formatting | bytes 3145728 | tf_op jit(solution)/shard_map/reshape | solution.py:106
  130.8 0.0 collective-permute-start.4
  130.8 3.7 %collective-permute-done.4 = bf16[768,1024]{1,0:T(8,128)(2,1)} collective-permute-done((bf16[768,1024]{1,0:T(8,128)(2,1)}, bf16[768,1024]{1,0:T(8,128)(2,1)}, u32[]{:S(2)}, u32[]{:S(2)}) %collective-permute-start.4) | collective-permute-done | bytes 1572896 | tf_op jit(solution)/shard_map/ppermute | solution.py:40
  134.5 2.1 broadcast_select_fusion.1
  136.7 1.2 copy-done.2
  137.9 0.4 copy-done.3
  138.3 2.8 %fusion.6 = f32[768,384]{1,0:T(8,128)} fusion(bf16[768,1024]{1,0:T(8,128)(2,1)S(1)} %get-tuple-element.8, bf16[768,1024]{1,0:T(8,128)(2,1)S(1)} %get-tuple-element.7, bf16[1,2048,384]{2,1,0:T(8,128)(2,1)S(1)} %copy-done.13), kind=kOutput, calls=%fused_computation.12 | convolution fusion | flops 1214251008 | bytes 5898240 | tf_op jit(solution)/shard_map/dot_general | solution.py:112
  141.1 9.3 %fusion.8 = f32[768,2048]{1,0:T(8,128)} fusion(bf16[1,384,2048]{2,1,0:T(8,128)(2,1)} %param.25, f32[768,384]{1,0:T(8,128)} %fusion.6, bf16[768,1024]{1,0:T(8,128)(2,1)} %copy-done.3, bf16[768,1024]{1,0:T(8,128)(2,1)} %copy-done.2, bf16[1,2048,384]{2,1,0:T(8,128)(2,1)} %param.23), kind=kOutput, calls=%fused_computation.15 | convolution fusion | flops 2423980032 | bytes 13762560 | tf_op jit(solution)/shard_map/dot_general | solution.py:114
  150.3 2.3 constant_dynamic-slice_fusion
  152.6 0.2 collective-permute-start.5
  152.8 5.5 %collective-permute-done.5 = f32[768,1024]{1,0:T(8,128)S(1)} collective-permute-done((f32[768,1024]{1,0:T(8,128)S(1)}, f32[768,1024]{1,0:T(8,128)S(1)}, u32[]{:S(2)}, u32[]{:S(2)}) %collective-permute-start.5) | collective-permute-done | bytes 3145760 | tf_op jit(solution)/shard_map/ppermute | solution.py:40
  158.4 1.7 add_convert_fusion
  160.0 3.7 %reshape.69 = bf16[128,6,1024]{2,1,0:T(8,128)(2,1)} reshape(bf16[768,1024]{1,0:T(8,128)(2,1)} %add_convert_fusion) | data formatting | bytes 3145728 | tf_op jit(solution)/shard_map/reshape | solution.py:119
  163.7 9.0 %all-to-all-start.2 = ((bf16[128,6,1024]{2,1,0:T(8,128)(2,1)}), bf16[128,6,1024]{2,1,0:T(8,128)(2,1)}, u32[]{:S(2)}, u32[]{:S(2)}) async-start(bf16[128,6,1024]{2,1,0:T(8,128)(2,1)} %reshape.69), calls=%async_computation.2 | async-start | bytes 4194304 | tf_op jit(solution)/shard_map/all_to_all | solution.py:118
  172.8 0.0 copy-done.11
  172.8 0.1 copy.53
  172.9 51.7 %all-to-all-done.2 = bf16[128,6,1024]{2,1,0:T(8,128)(2,1)} async-done(((bf16[128,6,1024]{2,1,0:T(8,128)(2,1)}), bf16[128,6,1024]{2,1,0:T(8,128)(2,1)}, u32[]{:S(2)}, u32[]{:S(2)}) %all-to-all-start.2) | async-done | bytes 1572896 | tf_op jit(solution)/shard_map/all_to_all | solution.py:118
  224.6 3.7 %reshape.73 = bf16[768,1024,1]{1,0,2:T(8,128)(2,1)} reshape(bf16[128,6,1024]{2,1,0:T(8,128)(2,1)} %all-to-all-done.2) | data formatting | bytes 3145728 | tf_op jit(solution)/shard_map/reshape | solution.py:124
  228.3 2.8 %multiply_reduce_fusion = f32[64,1024]{1,0:T(8,128)S(1)} fusion(bf16[768,1024,1]{1,0,2:T(8,128)(2,1)} %reshape.73, f32[64,8]{1,0:T(8,128)S(1)} %copy.53, s32[64,8]{1,0:T(8,128)S(1)} %copy.56), kind=kOutput, calls=%fused_computation.11 | convolution fusion | flops 806682624 | bytes 1839104 | tf_op jit(solution)/shard_map/tkr,rf->tkf/dot_general | solution.py:125
  231.1 0.7 add_convert_fusion.1
  (26 shorter events, 0.1 us)
Async XLA Ops:
  0.0 36.3 %copy-start = (bf16[2048,512]{1,0:T(8,128)(2,1)S(1)}, bf16[2048,512]{1,0:T(8,128)(2,1)}, u32[]{:S(2)}) copy-start(bf16[2048,512]{1,0:T(8,128)(2,1)} %param.18) | copy-start | bytes 6291460
  0.6 2.9 %copy-start.5 = (bf16[64,2048]{1,0:T(8,128)(2,1)S(1)}, bf16[64,2048]{1,0:T(8,128)(2,1)}, u32[]{:S(2)}) copy-start(bf16[64,2048]{1,0:T(8,128)(2,1)} %param.13) | copy-start | bytes 786436
  4.3 2.9 %copy-start.8 = (bf16[64,256]{1,0:T(8,128)(2,1)S(1)}, bf16[64,256]{1,0:T(8,128)(2,1)}, u32[]{:S(2)}) copy-start(bf16[64,256]{1,0:T(8,128)(2,1)} %param.15) | copy-start | bytes 98308
  4.3 2.9 %copy-start.9 = (bf16[64,256]{1,0:T(8,128)(2,1)S(1)}, bf16[64,256]{1,0:T(8,128)(2,1)}, u32[]{:S(2)}) copy-start(bf16[64,256]{1,0:T(8,128)(2,1)} %param.14) | copy-start | bytes 98308
  4.3 4.3 %copy-start.6 = (bf16[8,8,16,128]{3,2,1,0:T(8,128)(2,1)S(1)}, bf16[8,8,16,128]{3,2,1,0:T(8,128)(2,1)}, u32[]{:S(2)}) copy-start(bf16[8,8,16,128]{3,2,1,0:T(8,128)(2,1)} %copy.62) | copy-start | bytes 786436
  8.6 4.7 %copy-start.4 = (bf16[2048,2,128]{2,0,1:T(8,128)(2,1)S(1)}, bf16[2048,2,128]{2,0,1:T(8,128)(2,1)}, u32[]{:S(2)}) copy-start(bf16[2048,2,128]{2,0,1:T(8,128)(2,1)} %copy.48) | copy-start | bytes 3145732
  20.8 8.4 %collective-permute-start = (bf16[64,2048]{1,0:T(8,128)(2,1)}, bf16[64,2048]{1,0:T(8,128)(2,1)}, u32[]{:S(2)}, u32[]{:S(2)}) collective-permute-start(bf16[64,2048]{1,0:T(8,128)(2,1)} %bitcast.75), channel_id=1, source_target_pairs={{0,64},{64,128},{128,192},{192,0},{1,65},{65,129},{129,193},{193,1... | collective-permute-start | bytes 786440 | tf_op jit(solution)/shard_map/ppermute | solution.py:70
  22.3 9.4 %collective-permute-start.1 = (bf16[64,2048]{1,0:T(8,128)(2,1)}, bf16[64,2048]{1,0:T(8,128)(2,1)}, u32[]{:S(2)}, u32[]{:S(2)}) collective-permute-start(bf16[64,2048]{1,0:T(8,128)(2,1)} %bitcast.75), channel_id=1, source_target_pairs={{0,192},{64,0},{128,64},{192,128},{1,193},{65,1},{129,65},{193,129... | collective-permute-start | bytes 786440 | tf_op jit(solution)/shard_map/ppermute | solution.py:75
  29.1 7.2 %collective-permute-start.2 = (bf16[64,2048]{1,0:T(8,128)(2,1)}, bf16[64,2048]{1,0:T(8,128)(2,1)S(1)}, u32[]{:S(2)}, u32[]{:S(2)}) collective-permute-start(bf16[64,2048]{1,0:T(8,128)(2,1)} %collective-permute-done), channel_id=1, source_target_pairs={{0,64},{64,128},{128,192},{192,0},{1,65},{65,129},{129,193},{193,1... | collective-permute-start | bytes 786440 | tf_op jit(solution)/shard_map/ppermute | solution.py:70
  36.3 7.5 %copy-start.10 = (s32[64,8]{0,1:T(8,128)S(1)}, s32[64,8]{0,1:T(8,128)}, u32[]{:S(2)}) copy-start(s32[64,8]{0,1:T(8,128)} %param.21) | copy-start | bytes 6148
  37.8 14.6 %copy-start.12 = (f32[2048]{0:T(1024)S(1)}, f32[2048]{0:T(1024)}, u32[]{:S(2)}) copy-start(f32[2048]{0:T(1024)} %param.20) | copy-start | bytes 24580
  37.8 15.2 %copy-start.7 = (bf16[64,2048]{1,0:T(8,128)(2,1)S(1)}, bf16[64,2048]{1,0:T(8,128)(2,1)}, u32[]{:S(2)}) copy-start(bf16[64,2048]{1,0:T(8,128)(2,1)} %param.19) | copy-start | bytes 786436
  37.8 12.6 %all-to-all-start = ((f32[4,64,512]{2,1,0:T(8,128)}), f32[4,64,512]{2,1,0:T(8,128)S(1)}, u32[]{:S(2)}, u32[]{:S(2)}) async-start(f32[4,64,512]{2,1,0:T(8,128)} %bitcast.83), calls=%async_computation | async-start | bytes 1048576 | tf_op jit(solution)/shard_map/all_to_all | solution.py:81
  50.5 2.5 %collective-permute-start.3 = (f32[64,2048]{1,0:T(8,128)S(1)}, f32[64,2048]{1,0:T(8,128)}, u32[]{:S(2)}, u32[]{:S(2)}) collective-permute-start(f32[64,2048]{1,0:T(8,128)S(1)} %bitcast.81), channel_id=1, source_target_pairs={{0,1},{1,0},{2,3},{3,2},{4,5},{5,4},{6,7},{7,6},{8,9},{9,8},{10,11... | collective-permute-start | bytes 1572872 | tf_op jit(solution)/shard_map/ppermute | solution.py:40
  130.8 3.8 %collective-permute-start.4 = (bf16[768,1024]{1,0:T(8,128)(2,1)}, bf16[768,1024]{1,0:T(8,128)(2,1)}, u32[]{:S(2)}, u32[]{:S(2)}) collective-permute-start(bf16[768,1024]{1,0:T(8,128)(2,1)} %reshape.68), channel_id=1, source_target_pairs={{0,1},{1,0},{2,3},{3,2},{4,5},{5,4},{6,7},{7,6},{8,9},{9,8},{10,11... | collective-permute-start | bytes 4718600 | tf_op jit(solution)/shard_map/ppermute | solution.py:40
  130.8 7.5 %copy-start.13 = (bf16[1,2048,384]{2,1,0:T(8,128)(2,1)S(1)}, bf16[1,2048,384]{2,1,0:T(8,128)(2,1)}, u32[]{:S(2)}) copy-start(bf16[1,2048,384]{2,1,0:T(8,128)(2,1)} %param.24) | copy-start | bytes 4718596
  136.6 1.2 copy-start.2
  136.6 1.6 copy-start.3
  150.3 8.0 %copy-start.1 = (f32[768,2048]{1,0:T(8,128)S(1)}, f32[768,2048]{1,0:T(8,128)}, u32[]{:S(2)}) copy-start(f32[768,2048]{1,0:T(8,128)} %fusion.8) | copy-start | bytes 18874372
  152.6 5.7 %collective-permute-start.5 = (f32[768,1024]{1,0:T(8,128)S(1)}, f32[768,1024]{1,0:T(8,128)S(1)}, u32[]{:S(2)}, u32[]{:S(2)}) collective-permute-start(f32[768,1024]{1,0:T(8,128)S(1)} %constant_dynamic-slice_fusion), channel_id=1, source_target_pairs={{0,1},{1,0},{2,3},{3,2},{4,5},{5,4},{6,7},{7,6},{8,9},{9,8},{10,11... | collective-permute-start | bytes 9437192 | tf_op jit(solution)/shard_map/ppermute | solution.py:40
  163.7 9.0 %copy-start.11 = (f32[64,8]{0,1:T(8,128)S(1)}, f32[64,8]{0,1:T(8,128)}, u32[]{:S(2)}) copy-start(f32[64,8]{0,1:T(8,128)} %param.22) | copy-start | bytes 6148
  163.7 60.9 %all-to-all-start.2 = ((bf16[128,6,1024]{2,1,0:T(8,128)(2,1)}), bf16[128,6,1024]{2,1,0:T(8,128)(2,1)}, u32[]{:S(2)}, u32[]{:S(2)}) async-start(bf16[128,6,1024]{2,1,0:T(8,128)(2,1)} %reshape.69), calls=%async_computation.2 | async-start | bytes 4194304 | tf_op jit(solution)/shard_map/all_to_all | solution.py:118
